TPU v7x, 256 devices: a whole 4x4x8 slice. The times are simulated.
256 devices in a mesh: samp: 4 (over z_hi, core), vert: 64 (over x, z_lo, y).
Axes of the slice: x: 4, y: 4, z: 8 (z_hi: 2, z_lo: 4; z = z_hi * 4 + z_lo), core: 2. Of those that a mesh axis runs over, the one named last changes fastest.
Arguments:
- inputs: bfloat16 [8, 262144, 128], P('samp', 'vert'), may hold values from -6 to 6
- cotangent: bfloat16 [8, 262144, 128], P('samp', 'vert'), may hold values from -6 to 6
- basis: bfloat16 [262144, 1024], P('vert'), may hold values from -0.0234375 to 0.0234375
- mode_weights: bfloat16 [1024, 128, 128], P('vert'), may hold values from -0.5 to 0.5
- w_up: bfloat16 [128, 512], replicated, may hold values from -0.5 to 0.5
- b_up: float32 [512], replicated, may hold values from -4 to 4
- w_down: bfloat16 [512, 128], replicated, may hold values from -0.25 to 0.25
Outputs:
- grad_input: bfloat16 [8, 262144, 128], P('samp', 'vert')
- grad_modes: float32 [1024, 128, 128], P('vert')
- grad_w_up: float32 [128, 512], replicated
- grad_b_up: float32 [512], replicated
- grad_w_down: float32 [512, 128], replicated
All inputs are finite; a program needn't handle non-finite values.
Results may differ from a plain program's by a relative error of at most 0.0055.
Values may be sent and summed in bfloat16 or wider, within the bound.
No kernel may reach another device: no remote copies, remote signals or barrier semaphores. Data moves between devices by JAX's collectives and lax.ppermute only.
A program may use at most 128 MiB of HBM per device.

v0:
```python
import jax
import jax.numpy as jnp
from jax import lax
from jax.sharding import PartitionSpec as P


def gelu_value(pre_act):
    inner = 0.7978845608 * (pre_act + 0.044715 * pre_act * pre_act * pre_act)
    return 0.5 * pre_act * (1.0 + jnp.tanh(inner))


def gelu_slope(pre_act):
    inner = 0.7978845608 * (pre_act + 0.044715 * pre_act * pre_act * pre_act)
    tangent = jnp.tanh(inner)
    return 0.5 * (1.0 + tangent) + 0.5 * pre_act * (1.0 - tangent * tangent) * 0.7978845608 * (
        1.0 + 3.0 * 0.044715 * pre_act * pre_act
    )


def spectral_part(grad_out, mode_weights, basis):
    mixing = mode_weights.astype(jnp.float32)
    grad_coef = jnp.einsum(
        "skd,kcd->skc", grad_out, mixing, precision=lax.Precision.HIGHEST
    ).astype(jnp.bfloat16)
    return jnp.einsum(
        "vk,skc->svc",
        basis,
        lax.all_gather(grad_coef, "vert", axis=1, tiled=True),
        preferred_element_type=jnp.float32,
    )


def pointwise_part(inputs, cotangent, w_up, b_up, w_down):
    samples_here = inputs.shape[0]
    vertices_here = inputs.shape[1]
    channels = inputs.shape[2]
    flat_inputs = inputs.reshape(samples_here * vertices_here, channels)
    flat_cotangent = cotangent.reshape(samples_here * vertices_here, channels)
    pre_act = jnp.dot(flat_inputs, w_up, preferred_element_type=jnp.float32) + b_up
    hidden = gelu_value(pre_act).astype(jnp.bfloat16)
    grad_hidden = jnp.dot(flat_cotangent, w_down.T, preferred_element_type=jnp.float32)
    grad_pre = (grad_hidden * gelu_slope(pre_act)).astype(jnp.bfloat16)
    pointwise = jnp.dot(grad_pre, w_up.T, preferred_element_type=jnp.float32)
    local_up = jnp.dot(flat_inputs.T, grad_pre, preferred_element_type=jnp.float32)
    local_bias = jnp.sum(grad_pre.astype(jnp.float32), axis=0)
    local_down = jnp.dot(hidden.T, flat_cotangent, preferred_element_type=jnp.float32)
    sums = lax.psum((local_up, local_bias, local_down), ("samp", "vert"))
    return (pointwise.reshape(samples_here, vertices_here, channels), sums)


def per_device(inputs, cotangent, basis, mode_weights, w_up, b_up, w_down):
    channels = inputs.shape[2]
    stacked = jnp.concatenate([inputs, cotangent], axis=2)
    projected = jnp.einsum("vk,svc->skc", basis, stacked, preferred_element_type=jnp.float32)
    owned_sums = lax.psum_scatter(projected, "vert", scatter_dimension=1, tiled=True)
    coeffs = owned_sums[:, :, :channels]
    grad_out = owned_sums[:, :, channels:]
    spectral = spectral_part(grad_out, mode_weights, basis)
    pointwise, mlp_grads = pointwise_part(inputs, cotangent, w_up, b_up, w_down)
    local_modes = jnp.einsum("skc,skd->kcd", coeffs, grad_out, precision=lax.Precision.HIGHEST)
    grad_modes = lax.psum(local_modes, "samp")
    grad_input = (spectral + pointwise).astype(jnp.bfloat16)
    grad_w_up, grad_b_up, grad_w_down = mlp_grads
    return (grad_input, grad_modes, grad_w_up, grad_b_up, grad_w_down)


def solution(mesh):
    in_specs = (
        P("samp", "vert", None),
        P("samp", "vert", None),
        P("vert", None),
        P("vert", None, None),
        P(),
        P(),
        P(),
    )
    out_specs = (P("samp", "vert", None), P("vert", None, None), P(), P(), P())
    return jax.shard_map(
        per_device, mesh=mesh, in_specs=in_specs, out_specs=out_specs, check_vma=False
    )
```

profile of v0, /device:TPU:0, one launch (start us, length us, event | category | flops | bytes accessed | tf_op | source)
XLA Modules:
  0.0 1230.6 jit_solution(3378659776492930055)
XLA Ops:
  7.2 0.0 copy-start
  7.2 0.0 all-reduce.10.cloned.1.call-start
  7.2 0.0 copy-start.2
  7.2 0.0 copy-start.6
  7.2 4.1 fusion.42
  11.3 0.0 copy-done.2
  11.3 0.0 copy-done.6
  11.3 0.0 copy-start.5
  11.4 7.7 fusion.11
  19.1 0.0 copy-done.5
  19.1 0.0 copy-start.1
  19.1 15.0 %convert_reduce_fusion = (f32[512]{0:T(512)S(1)}, bf16[8192,512]{1,0:T(8,128)(2,1)}) fusion(f32[8192,512]{1,0:T(8,128)S(1)} %fusion.42, f32[512]{0:T(512)S(1)} %copy-done.6, bf16[8192,128]{1,0:T(8,128)(2,1)} %bitcast.42, bf16[512,128]{1,0:T(8,128)(2,1)S(1)} %copy-done.5), kind=kOutput, calls=%fused_computation.10 | convolution fusion | flops 1166016000 | bytes 27398144 | tf_op jit(solution)/shard_map/dot_general | solution.py:41
  34.1 0.0 copy-done.1
  34.1 6.4 convolution_bitcast_fusion
  40.5 0.0 all-reduce.10.cloned.1.call-update
  40.6 0.2 all-reduce.8.cloned.1.call-start
  40.8 2.8 copy.32
  43.6 4.1 copy.33
  47.7 0.0 copy-start.3
  47.7 8.2 fusion.24
  55.9 2.3 copy.34
  58.2 0.0 all-reduce.8.cloned.1.call-update
  58.2 0.0 all-reduce.6.cloned.1.call-start
  58.3 0.0 copy-done.3
  58.3 7.7 fusion.43
  66.0 0.0 copy-start.7
  66.0 5.7 copy.36
  71.7 0.0 copy-done.7
  71.7 0.6 dynamic-slice
  72.9 79.6 %psum.30 = f32[512]{0:T(512)} all-reduce(f32[512]{0:T(512)S(1)} %get-tuple-element.27), channel_id=1, replica_groups=mesh['samp'=4,'vert'=64] {'samp','vert'}, use_global_device_ids=true, to_apply=%region_4.0 | all-reduce | flops 512 | bytes 4096 | tf_op jit(solution)/shard_map/psum | solution.py:47
  152.5 142.1 %all-reduce.10.cloned.1.call-done = (f32[128,512]{0,1:T(8,128)}, f32[512,128]{1,0:T(8,128)}) async-done(((f32[128,512]{0,1:T(8,128)}, f32[512,128]{1,0:T(8,128)}), (f32[128,512]{0,1:T(8,128)}, f32[512,128]{1,0:T(8,128)})) %all-reduce.10.cloned.1.call-update) | async-done | bytes 524304 | tf_op jit(solution)/shard_map/psum | solution.py:47
  294.5 1.8 copy.38
  296.3 717.1 %all-reduce.8.cloned.1.call-done = f32[2,1024,256]{2,0,1:T(2,128)} async-done(((f32[2,1024,256]{2,0,1:T(2,128)}), f32[2,1024,256]{2,0,1:T(2,128)}) %all-reduce.8.cloned.1.call-update) | async-done | bytes 2097168
  1013.5 3.5 fusion.31
  1017.0 0.0 all-reduce.6.cloned.1.call-update
  1017.0 0.0 copy-done
  1017.0 1.7 fusion.29
  1018.7 192.9 %all_gather.3 = bf16[2,1024,128]{2,0,1:T(2,128)(2,1)S(1)} all-gather(bf16[2,16,128]{2,0,1:T(2,128)(2,1)S(1)} %fusion.29), channel_id=1, replica_groups=mesh['samp'=4,'vert'=64] {'vert'}, dimensions={1}, use_global_device_ids=true | all-gather | bytes 532480 | tf_op jit(solution)/shard_map/all_gather | solution.py:28
  1211.6 0.0 copy-start.4
  1211.6 7.0 fusion.18
  1218.6 2.5 copy.37
  1221.1 0.0 all-reduce.6.cloned.1.call-done
  1221.1 2.3 copy.45
  1223.4 0.0 copy-done.4
  1223.4 0.7 copy.46
Async XLA Ops:
  7.2 1009.9 %copy-start = (bf16[16,128,128]{2,1,0:T(8,128)(2,1)S(1)}, bf16[16,128,128]{2,1,0:T(8,128)(2,1)}, u32[]{:S(2)}) copy-start(bf16[16,128,128]{2,1,0:T(8,128)(2,1)} %param.10) | copy-start | bytes 1572868
  7.2 287.4 %all-reduce.10.cloned.1.call-start = ((), (), s32[]{:S(2)}) async-start(), calls=%async_computation.2 | async-start | bytes 1048576 | tf_op jit(solution)/shard_map/psum | solution.py:47
  7.2 4.1 copy-start.2
  7.2 4.1 copy-start.6
  11.3 7.7 copy-start.5
  19.1 15.0 %copy-start.1 = (bf16[2,4096,128]{2,1,0:T(8,128)(2,1)S(1)}, bf16[2,4096,128]{2,1,0:T(8,128)(2,1)}, u32[]{:S(2)}) copy-start(bf16[2,4096,128]{2,1,0:T(8,128)(2,1)} %param.7) | copy-start | bytes 6291460
  40.6 972.9 %all-reduce.8.cloned.1.call-start = ((), (), s32[]{:S(2)}) async-start(), calls=%async_computation.1 | async-start | bytes 4194304
  47.7 10.6 copy-start.3
  58.2 1162.9 %all-reduce.6.cloned.1.call-start = ((), (), s32[]{:S(2)}) async-start(), calls=%async_computation | async-start | bytes 2097152 | tf_op jit(solution)/shard_map/psum | solution.py:61
  66.0 5.7 copy-start.7
  1211.6 11.8 copy-start.4
Sparse Core Ops, SparseCore 0:
  40.7 253.8 all-reduce.9
  297.7 715.6 all-reduce.7
  1017.1 68.9 all-reduce.5
where the time goes:
time: 1230 us
  waiting for transfers between devices  859 us (70%)
  blocking collectives  272 us (22%)
  matrix products  61.4 us (5%)
  local copies, waits for them, and re-layouts  22.7 us (2%)
  between operations  14.5 us (1%)
    unnamed x4, waiting for transfers between devices  717 us
    all_gather x1, blocking collectives, spectral_part(): lax.all_gather(grad_coef, 'vert', axis=1, tiled=True)  193 us
    psum x1, waiting for transfers between devices, pointwise_part(): sums = lax.psum((local_up, local_bias, local_down), ('samp', 'vert'))  142 us
    psum x1, blocking collectives, pointwise_part(): sums = lax.psum((local_up, local_bias, local_down), ('samp', 'vert'))  79.6 us
  transfers between devices with their start and end apart: 3, of which 2 were waited for; matrix products, arithmetic and copies ran while one was open for 4% of the time, Pallas kernels for 0%

commit v1 on v0

--- a/solution.py
+++ b/solution.py
@@ -2,6 +2,7 @@
 import jax.numpy as jnp
 from jax import lax
 from jax.sharding import PartitionSpec as P
+from jax.lax import psum
 
 
 def gelu_value(pre_act):
@@ -44,7 +45,9 @@
     local_up = jnp.dot(flat_inputs.T, grad_pre, preferred_element_type=jnp.float32)
     local_bias = jnp.sum(grad_pre.astype(jnp.float32), axis=0)
     local_down = jnp.dot(hidden.T, flat_cotangent, preferred_element_type=jnp.float32)
-    sums = lax.psum((local_up, local_bias, local_down), ("samp", "vert"))
+    sums = (local_up, local_bias, local_down)
+    for rr in ("samp", "vert"):
+        sums = psum(sums, rr)
     return (pointwise.reshape(samples_here, vertices_here, channels), sums)
 
 

time: 1230 us -> 1040 us (0.85)
  waiting for transfers between devices: 859 us -> 549 us
  blocking collectives: 272 us -> 390 us
    unnamed x4, waiting for transfers between devices: 717 us -> 508 us
    psum x1 -> x2, blocking collectives: 79.6 us -> 199 us  [pointwise_part(): sums = psum(sums, rr)]
    psum x1, waiting for transfers between devices: 142 us -> 41.7 us  [pointwise_part(): sums = psum(sums, rr)]
where the time goes in v1:
time: 1040 us
  waiting for transfers between devices  549 us (53%)
  blocking collectives  390 us (38%)
  matrix products  61.4 us (6%)
  local copies, waits for them, and re-layouts  21.8 us (2%)
  between operations  14.5 us (1%)
    unnamed x4, waiting for transfers between devices  508 us
    psum x2, blocking collectives, pointwise_part(): sums = psum(sums, rr)  199 us
    all_gather x1, blocking collectives, spectral_part(): lax.all_gather(grad_coef, 'vert', axis=1, tiled=True)  191 us
    psum x1, waiting for transfers between devices, pointwise_part(): sums = psum(sums, rr)  41.7 us
  transfers between devices with their start and end apart: 3, of which 2 were waited for; matrix products, arithmetic and copies ran while one was open for 4% of the time, Pallas kernels for 0%

profile of v1, /device:TPU:0, one launch (start us, length us, event | category | flops | bytes accessed | tf_op | source)
XLA Modules:
  0.0 1037.1 jit_solution(10023099710026586386)
XLA Ops:
  7.2 0.0 copy-start
  7.2 0.0 all-reduce.11.cloned.1.call-start
  7.2 0.0 copy-start.2
  7.2 0.0 copy-start.7
  7.2 4.1 fusion.42
  11.3 0.0 copy-done.2
  11.3 0.0 copy-done.7
  11.3 0.0 copy-start.6
  11.4 7.7 fusion.11
  19.1 0.0 copy-done.6
  19.1 0.0 copy-start.1
  19.1 15.0 %convert_reduce_fusion = (f32[512]{0:T(512)S(1)}, bf16[8192,512]{1,0:T(8,128)(2,1)}) fusion(f32[8192,512]{1,0:T(8,128)S(1)} %fusion.42, f32[512]{0:T(512)S(1)} %copy-done.7, bf16[8192,128]{1,0:T(8,128)(2,1)} %bitcast.42, bf16[512,128]{1,0:T(8,128)(2,1)S(1)} %copy-done.6), kind=kOutput, calls=%fused_computation.10 | convolution fusion | flops 1166016000 | bytes 27398144 | tf_op jit(solution)/shard_map/dot_general | solution.py:42
  34.1 0.0 copy-done.1
  34.1 6.4 convolution_bitcast_fusion
  40.5 0.0 all-reduce.11.cloned.1.call-update
  40.6 0.2 all-reduce.9.cloned.1.call-start
  40.8 2.8 copy.32
  43.6 4.1 copy.33
  47.7 0.0 copy-start.3
  47.7 8.2 fusion.24
  55.9 2.3 copy.34
  58.2 41.7 %all-reduce.11.cloned.1.call-done = (f32[128,512]{0,1:T(8,128)}, f32[512,128]{1,0:T(8,128)}) async-done(((f32[128,512]{0,1:T(8,128)}, f32[512,128]{1,0:T(8,128)}), (f32[128,512]{0,1:T(8,128)}, f32[512,128]{1,0:T(8,128)})) %all-reduce.11.cloned.1.call-update) | async-done | bytes 524304 | tf_op jit(solution)/shard_map/psum | solution.py:50
  99.9 0.0 all-reduce.9.cloned.1.call-update
  99.9 0.0 all-reduce.7.cloned.1.call-start
  100.0 0.0 copy-done.3
  100.0 7.7 fusion.43
  107.7 0.0 copy-start.8
  107.7 5.6 copy.36
  113.3 0.0 copy-done.8
  113.3 0.6 dynamic-slice
  114.6 12.1 %psum.52 = f32[512]{0:T(512)S(1)} all-reduce(f32[512]{0:T(512)S(1)} %get-tuple-element.30), channel_id=1, replica_groups=mesh['samp'=4,'vert'=64] {'samp'}, use_global_device_ids=true, to_apply=%region_5.0 | all-reduce | flops 512 | bytes 4096 | tf_op jit(solution)/shard_map/psum | solution.py:50
  126.7 187.0 %psum.53 = f32[512]{0:T(512)} all-reduce(f32[512]{0:T(512)S(1)} %psum.52), channel_id=1, replica_groups=mesh['samp'=4,'vert'=64] {'vert'}, use_global_device_ids=true, to_apply=%region_6.0 | all-reduce | flops 512 | bytes 4096 | tf_op jit(solution)/shard_map/psum | solution.py:50
  313.7 507.6 %all-reduce.9.cloned.1.call-done = (f32[2,1024,256]{2,0,1:T(2,128)}, f32[128,512]{0,1:T(8,128)}, f32[512,128]{1,0:T(8,128)}) async-done(((f32[2,1024,256]{2,0,1:T(2,128)}, f32[128,512]{0,1:T(8,128)}, f32[512,128]{1,0:T(8,128)}), (f32[2,1024,256]{2,0,1:T(2,128)}, f32[128,512]{0,1:T(8,128)}, f32[512,128]{1,0:T(8,128)})) %all-reduce.9.cloned.1.call-update) | async-done | bytes 2621456
  821.3 3.5 fusion.31
  824.8 0.0 copy-done
  824.8 1.7 fusion.29
  826.5 0.0 all-reduce.7.cloned.1.call-update
  826.5 190.7 %all_gather.3 = bf16[2,1024,128]{2,0,1:T(2,128)(2,1)S(1)} all-gather(bf16[2,16,128]{2,0,1:T(2,128)(2,1)S(1)} %fusion.29), channel_id=1, replica_groups=mesh['samp'=4,'vert'=64] {'vert'}, dimensions={1}, use_global_device_ids=true | all-gather | bytes 532480 | tf_op jit(solution)/shard_map/all_gather | solution.py:29
  1017.2 0.0 copy-start.5
  1017.2 0.0 copy-start.4
  1017.2 7.0 fusion.18
  1024.3 2.5 copy.37
  1026.7 0.0 copy-done.5
  1026.7 0.8 copy.38
  1027.6 0.0 all-reduce.7.cloned.1.call-done
  1027.6 2.3 copy.47
  1029.9 0.0 copy-done.4
  1029.9 0.7 copy.48
Async XLA Ops:
  7.2 817.7 %copy-start = (bf16[16,128,128]{2,1,0:T(8,128)(2,1)S(1)}, bf16[16,128,128]{2,1,0:T(8,128)(2,1)}, u32[]{:S(2)}) copy-start(bf16[16,128,128]{2,1,0:T(8,128)(2,1)} %param.10) | copy-start | bytes 1572868
  7.2 92.7 %all-reduce.11.cloned.1.call-start = ((), (), s32[]{:S(2)}) async-start(), calls=%async_computation.2 | async-start | bytes 1048576 | tf_op jit(solution)/shard_map/psum | solution.py:50
  7.2 4.1 copy-start.2
  7.2 4.1 copy-start.7
  11.3 7.7 copy-start.6
  19.1 15.0 %copy-start.1 = (bf16[2,4096,128]{2,1,0:T(8,128)(2,1)S(1)}, bf16[2,4096,128]{2,1,0:T(8,128)(2,1)}, u32[]{:S(2)}) copy-start(bf16[2,4096,128]{2,1,0:T(8,128)(2,1)} %param.7) | copy-start | bytes 6291460
  40.6 780.7 %all-reduce.9.cloned.1.call-start = ((), (), s32[]{:S(2)}) async-start(), calls=%async_computation.1 | async-start | bytes 5242880
  47.7 52.3 %copy-start.3 = (bf16[128,512]{1,0:T(8,128)(2,1)S(1)}, bf16[128,512]{1,0:T(8,128)(2,1)}, u32[]{:S(2)}) copy-start(bf16[128,512]{1,0:T(8,128)(2,1)} %param.11) | copy-start | bytes 393220
  99.9 927.6 %all-reduce.7.cloned.1.call-start = ((), (), s32[]{:S(2)}) async-start(), calls=%async_computation | async-start | bytes 2097152 | tf_op jit(solution)/shard_map/psum | solution.py:64
  107.7 5.6 copy-start.8
  1017.2 9.5 copy-start.5
  1017.2 12.6 %copy-start.4 = (f32[512,128]{1,0:T(8,128)S(1)}, f32[512,128]{1,0:T(8,128)}, u32[]{:S(2)}) copy-start(f32[512,128]{1,0:T(8,128)} %get-tuple-element.36) | copy-start | bytes 786436
Sparse Core Ops, SparseCore 0:
  40.7 59.1 all-reduce.10
  103.3 717.9 all-reduce.8
  826.7 69.1 all-reduce.6

commit v2 on v0

--- a/solution.py
+++ b/solution.py
@@ -2,6 +2,13 @@
 import jax.numpy as jnp
 from jax import lax
 from jax.sharding import PartitionSpec as P
+
+
+def exchange_gather(x, mesh_axis, dim):
+    size = lax.axis_size(mesh_axis)
+    pieces = jnp.stack([x for _ in range(size)])
+    pieces = lax.all_to_all(pieces, mesh_axis, split_axis=0, concat_axis=0)
+    return jnp.concatenate(pieces, axis=dim)
 
 
 def gelu_value(pre_act):
@@ -25,7 +32,7 @@
     return jnp.einsum(
         "vk,skc->svc",
         basis,
-        lax.all_gather(grad_coef, "vert", axis=1, tiled=True),
+        exchange_gather(grad_coef, "vert", 1),
         preferred_element_type=jnp.float32,
     )
 

time: 1230 us -> 1110 us (0.902)
  blocking collectives: 272 us -> 77.1 us
  waiting for transfers between devices: 859 us -> 902 us
    all_gather x1 -> x0, blocking collectives: 193 us -> none  [spectral_part(): lax.all_gather(grad_coef, 'vert', axis=1, tiled=True)]
    psum x1, waiting for transfers between devices: 0.01 us -> 61.3 us  [per_device(): grad_modes = lax.psum(local_modes, 'samp')]
    unnamed x4, waiting for transfers between devices: 717 us -> 683 us
    psum x1, waiting for transfers between devices: 142 us -> 158 us  [pointwise_part(): sums = lax.psum((local_up, local_bias, local_down), ('samp', 'vert'))]
  transfers between devices with their start and end apart: 3 -> 4, of which waited for: 2 -> 3; matrix products, arithmetic and copies ran while one was open for 4% -> 6% of each run, Pallas kernels for 0% -> 0%
where the time goes in v2:
time: 1110 us; the launch traced here: 1100 us
  waiting for transfers between devices  902 us (81%)
  blocking collectives  77.1 us (7%)
  matrix products  70.6 us (6%)
  local copies, waits for them, and re-layouts  26.8 us (2%)
  between operations  16.3 us (1%)
    unnamed x4, waiting for transfers between devices  683 us
    psum x1, waiting for transfers between devices, pointwise_part(): sums = lax.psum((local_up, local_bias, local_down), ('samp', 'vert'))  158 us
    psum x1, blocking collectives, pointwise_part(): sums = lax.psum((local_up, local_bias, local_down), ('samp', 'vert'))  77.1 us
    psum x1, waiting for transfers between devices, per_device(): grad_modes = lax.psum(local_modes, 'samp')  61.3 us
  transfers between devices with their start and end apart: 4, of which 3 were waited for; matrix products, arithmetic and copies ran while one was open for 6% of the time, Pallas kernels for 0%

profile of v2, /device:TPU:0, one launch (start us, length us, event | category | flops | bytes accessed | tf_op | source)
XLA Modules:
  0.0 1103.0 jit_solution(9852572421213501928)
XLA Ops:
  8.0 0.0 copy-start
  8.0 0.0 all-reduce.8.cloned.1.call-start
  8.1 4.2 copy.30
  12.2 4.1 copy.31
  16.3 0.0 copy-start.2
  16.3 0.0 copy-start.3
  16.3 10.6 fusion.24
  26.9 4.1 copy.32
  31.0 0.0 all-reduce.8.cloned.1.call-update
  31.0 0.0 copy-done.2
  31.1 0.0 copy-done.3
  31.1 0.0 copy-start.7
  31.1 0.0 copy-start.5
  31.1 0.0 copy-start.6
  31.1 8.1 fusion.41
  39.2 0.0 copy-done.7
  39.2 0.6 dynamic-slice
  40.4 0.0 copy-done.5
  40.4 0.0 copy-done.6
  40.4 0.0 copy-start.1
  40.4 17.4 %convert_reduce_fusion = (f32[512]{0:T(512)S(1)}, bf16[8192,512]{1,0:T(8,128)(2,1)}) fusion(f32[8192,512]{1,0:T(8,128)} %fusion.41, f32[512]{0:T(512)S(1)} %copy-done.6, bf16[8192,128]{1,0:T(8,128)(2,1)} %bitcast.46, bf16[512,128]{1,0:T(8,128)(2,1)S(1)} %copy-done.5), kind=kOutput, calls=%fused_computation.10 | convolution fusion | flops 1166016000 | bytes 27398144 | tf_op jit(solution)/shard_map/dot_general | solution.py:48
  57.8 0.0 copy-done.1
  57.8 8.2 fusion.11
  66.0 682.6 %all-reduce.8.cloned.1.call-done = f32[2,1024,256]{2,0,1:T(2,128)} async-done(((f32[2,1024,256]{2,0,1:T(2,128)}), f32[2,1024,256]{2,0,1:T(2,128)}) %all-reduce.8.cloned.1.call-update) | async-done | bytes 2097168
  748.6 0.0 copy-done
  748.6 1.7 fusion.29
  750.3 0.9 stack.2
  751.1 9.6 all-to-all-start
  760.8 0.0 all-reduce.10.cloned.1.call-start
  760.8 6.4 convolution_bitcast_fusion
  767.3 0.0 all-reduce.10.cloned.1.call-update
  767.3 0.3 all-reduce.6.cloned.1.call-start
  767.6 3.6 fusion.30
  771.1 0.0 all-reduce.6.cloned.1.call-update
  771.2 7.7 fusion.42
  778.8 5.7 copy.36
  784.5 77.1 %psum.30 = f32[512]{0:T(512)} all-reduce(f32[512]{0:T(512)S(1)} %get-tuple-element.22), channel_id=1, replica_groups=mesh['samp'=4,'vert'=64] {'samp','vert'}, use_global_device_ids=true, to_apply=%region_4.0 | all-reduce | flops 512 | bytes 4096 | tf_op jit(solution)/shard_map/psum | solution.py:54
  861.6 158.3 %all-reduce.10.cloned.1.call-done = (f32[128,512]{0,1:T(8,128)}, f32[512,128]{1,0:T(8,128)}) async-done(((f32[128,512]{0,1:T(8,128)}, f32[512,128]{1,0:T(8,128)}), (f32[128,512]{0,1:T(8,128)}, f32[512,128]{1,0:T(8,128)})) %all-reduce.10.cloned.1.call-update) | async-done | bytes 524304 | tf_op jit(solution)/shard_map/psum | solution.py:54
  1019.9 1.8 copy.38
  1021.7 0.0 all-to-all-done
  1021.7 0.0 copy-start.4
  1021.7 7.1 fusion.18
  1028.8 2.5 copy.37
  1031.3 61.3 %all-reduce.6.cloned.1.call-done = f32[16,128,128]{2,1,0:T(8,128)} async-done(((f32[16,128,128]{2,1,0:T(8,128)}), f32[16,128,128]{2,1,0:T(8,128)}) %all-reduce.6.cloned.1.call-update) | async-done | bytes 1048592 | tf_op jit(solution)/shard_map/psum | solution.py:68
  1092.6 2.3 copy.44
  1094.9 0.0 copy-done.4
  1094.9 0.7 copy.45
  (2 shorter events, 0.0 us)
Async XLA Ops:
  8.0 740.6 %copy-start = (bf16[16,128,128]{2,1,0:T(8,128)(2,1)S(1)}, bf16[16,128,128]{2,1,0:T(8,128)(2,1)}, u32[]{:S(2)}) copy-start(bf16[16,128,128]{2,1,0:T(8,128)(2,1)} %param.10) | copy-start | bytes 1572868
  8.0 740.6 %all-reduce.8.cloned.1.call-start = ((), (), s32[]{:S(2)}) async-start(), calls=%async_computation.2 | async-start | bytes 4194304
  16.3 14.7 %copy-start.2 = (bf16[2,4096,128]{2,1,0:T(8,128)(2,1)S(1)}, bf16[2,4096,128]{2,1,0:T(8,128)(2,1)}, u32[]{:S(2)}) copy-start(bf16[2,4096,128]{2,1,0:T(8,128)(2,1)} %param.7) | copy-start | bytes 6291460
  16.3 14.7 %copy-start.3 = (bf16[128,512]{1,0:T(8,128)(2,1)S(1)}, bf16[128,512]{1,0:T(8,128)(2,1)}, u32[]{:S(2)}) copy-start(bf16[128,512]{1,0:T(8,128)(2,1)} %param.11) | copy-start | bytes 393220
  31.1 8.1 copy-start.7
  31.1 9.3 copy-start.5
  31.1 9.3 copy-start.6
  40.4 17.4 %copy-start.1 = (f32[8192,512]{1,0:T(8,128)S(1)}, f32[8192,512]{1,0:T(8,128)}, u32[]{:S(2)}) copy-start(f32[8192,512]{1,0:T(8,128)} %fusion.41) | copy-start | bytes 50331652
  751.1 270.5 %all-to-all-start = ((bf16[64,2,16,128]{3,2,1,0:T(8,128)(2,1)}), bf16[64,2,16,128]{3,2,1,0:T(8,128)(2,1)S(1)}, u32[]{:S(2)}, u32[]{:S(2)}) async-start(bf16[64,2,16,128]{3,2,1,0:T(8,128)(2,1)} %stack.2), calls=%async_computation | async-start | bytes 1048576 | tf_op jit(solution)/shard_map/all_to_all | solution.py:10
  760.8 259.1 %all-reduce.10.cloned.1.call-start = ((), (), s32[]{:S(2)}) async-start(), calls=%async_computation.3 | async-start | bytes 1048576 | tf_op jit(solution)/shard_map/psum | solution.py:54
  767.3 325.3 %all-reduce.6.cloned.1.call-start = ((), (), s32[]{:S(2)}) async-start(), calls=%async_computation.1 | async-start | bytes 2097152 | tf_op jit(solution)/shard_map/psum | solution.py:68
  1021.7 73.2 %copy-start.4 = (f32[512,128]{1,0:T(8,128)S(1)}, f32[512,128]{1,0:T(8,128)}, u32[]{:S(2)}) copy-start(f32[512,128]{1,0:T(8,128)} %get-tuple-element.28) | copy-start | bytes 786436
Sparse Core Ops, SparseCore 0:
  31.2 717.3 all-reduce.7
Sparse Core Ops, SparseCore 1:
  768.4 251.4 all-reduce.9
  1023.2 69.4 all-reduce.5
